TPU v7x, 32 devices: a whole 2x2x4 slice. The times are simulated.
32 devices in a mesh: section: 2 (over core), dom: 16 (over z, y, x).
Axes of the slice: x: 2, y: 2, z: 4, core: 2. Of those that a mesh axis runs over, the one named last changes fastest.
Arguments:
- blocks: float32 [16, 32, 6, 128, 128], P('section', 'dom'), may hold values from -0.21875 to 0.21875
- column_index: int32 [16, 32, 6], P('section', 'dom'), may hold values from 0 to 31
- block_period: int32 [16, 32, 6], P('section', 'dom'), may hold values from 0 to 15, as said below
- cost_vector: float32 [16, 4096], P('section', 'dom'), may hold values from -6 to 6
- demand: float32 [16, 4096], P('section', 'dom'), may hold values from -12 to 12
- primal_start: float32 [16, 4096], P('section', 'dom'), may hold values from 0 to 2
- dual_start: float32 [16, 4096], P('section', 'dom'), may hold values from -3 to 3
- primal_weight: float32 [1], replicated, may hold values from 0.5 to 2
Outputs:
- primal_final: float32 [16, 4096], P('section', 'dom')
- dual_final: float32 [16, 4096], P('section', 'dom')
Inputs may be any that keep to these rules, and one draw needn't show every extreme that they name: block_period[p, r, k] is p or p - 1; it is p for k = 0 and for p = 0.
All inputs are finite; a program needn't handle non-finite values.
Results may differ from a plain program's by a relative error of at most 0.00011.
Values sent between devices are 32-bit elements; how exact they have to be, the bound alone decides.
A program may use at most 64 MiB of HBM per device.

v0:
```python
import jax
import jax.numpy as jnp
from jax import lax
from jax.sharding import PartitionSpec as P

step_scale = 0.4
epsilon = 1e-06


def passed_along(block, axis, distance):
    devices = range(lax.axis_size(axis))
    route = [(i - distance, i) for i in devices if i - distance in devices]
    return lax.ppermute(block, axis, route)


def slot_layout(column_index, block_period):
    periods_here = column_index.shape[0]
    local_period = jnp.arange(periods_here, dtype=jnp.int32)[:, None, None]
    global_period = lax.axis_index("section") * periods_here + local_period
    slot_index = local_period + block_period - global_period + 1
    return slot_index


def forward(blocks, column_index, slot_index, field):
    periods_here = field.shape[0]
    width_here = blocks.shape[-1]
    gathered = lax.all_gather(field, "dom", axis=1, tiled=True)
    carried = passed_along(gathered[-1:], "section", 1)
    stacked = jnp.concatenate([carried, gathered], axis=0)
    block_count = stacked.shape[1] // width_here
    picked = stacked.reshape(periods_here + 1, block_count, width_here)[slot_index, column_index]
    product = jnp.einsum("prkij,prkj->pri", blocks, picked, precision=lax.Precision.HIGHEST)
    return product.reshape(periods_here, -1)


def adjoint(blocks, column_index, slot_index, field):
    periods_here = field.shape[0]
    rows_here = blocks.shape[1]
    width_here = blocks.shape[-1]
    block_count = rows_here * lax.axis_size("dom")
    field_blocks = field.reshape(periods_here, rows_here, width_here)
    block_terms = jnp.einsum(
        "prkij,pri->prkj", blocks, field_blocks, precision=lax.Precision.HIGHEST
    )
    segment_ids = (slot_index * block_count + column_index).reshape(-1)
    dense_term = jax.ops.segment_sum(
        block_terms.reshape(-1, width_here),
        segment_ids,
        num_segments=(periods_here + 1) * block_count,
    )
    dense_term = dense_term.reshape(periods_here + 1, block_count * width_here)
    carried = passed_along(dense_term[:1], "section", -1)
    own_rows = dense_term[1:]
    merged = own_rows + jnp.concatenate([jnp.zeros_like(own_rows[:-1]), carried], axis=0)
    result = lax.psum_scatter(merged, "dom", scatter_dimension=1, tiled=True)
    return result


def on_device(
    blocks, column_index, block_period, cost_vector, demand, primal_start, dual_start, primal_weight
):
    slot_index = slot_layout(column_index, block_period)
    weight_now = primal_weight[0]
    tau_first = step_scale / weight_now
    sigma_first = step_scale * weight_now
    primal_one = jnp.maximum(
        0.0,
        primal_start
        - tau_first * (cost_vector - adjoint(blocks, column_index, slot_index, dual_start)),
    )
    dual_one = dual_start + sigma_first * (
        demand - forward(blocks, column_index, slot_index, 2.0 * primal_one - primal_start)
    )
    local_primal = jnp.sum((primal_one - primal_start) ** 2)
    local_dual = jnp.sum((dual_one - dual_start) ** 2)
    move_primal, move_dual = lax.psum((local_primal, local_dual), ("section", "dom"))
    weight_next = jnp.sqrt(weight_now * jnp.sqrt((move_dual + epsilon) / (move_primal + epsilon)))
    tau_second = step_scale / weight_next
    sigma_second = step_scale * weight_next
    primal_final = jnp.maximum(
        0.0,
        primal_one
        - tau_second * (cost_vector - adjoint(blocks, column_index, slot_index, dual_one)),
    )
    dual_final = dual_one + sigma_second * (
        demand - forward(blocks, column_index, slot_index, 2.0 * primal_final - primal_one)
    )
    return (primal_final, dual_final)


def solution(mesh):
    return jax.shard_map(
        on_device,
        mesh=mesh,
        in_specs=(
            P("section", "dom", None, None, None),
            P("section", "dom", None),
            P("section", "dom", None),
            P("section", "dom"),
            P("section", "dom"),
            P("section", "dom"),
            P("section", "dom"),
            P(),
        ),
        out_specs=(P("section", "dom"), P("section", "dom")),
        check_vma=False,
    )
```

profile of v0, /device:TPU:0, one launch (start us, length us, event | category | flops | bytes accessed | tf_op | source)
XLA Modules:
  0.0 288.4 jit_solution(15570511346201908841)
XLA Ops:
  7.2 0.7 fusion.14
  8.2 6.1 %fusion.10 = f32[8,2,1,6,128]{4,2,3,1,0:T(1,128)S(1)} fusion(f32[8,2,6,128,128]{4,3,2,1,0:T(8,128)} %param.8, f32[8,2,128,1,1]{2,0,1,3,4:T(8,128)} %bitcast.58), kind=kOutput, calls=%fused_computation.24 | convolution fusion | flops 18874368 | bytes 6348800 | tf_op jit(solution)/shard_map/prkij,pri->prkj/dot_general | solution.py:42
  14.3 0.9 scatter_custom_fusion
  15.2 1.3 collective-permute-start
  16.6 1.7 collective-permute-done
  18.3 0.7 pad_add_fusion.1
  19.8 78.9 %reduce-scatter.3.cloned.1.call-done = f32[8,256]{1,0:T(8,128)} async-done(((f32[8,4096]{1,0:T(8,128)}), f32[8,256]{1,0:T(8,128)}) %reduce-scatter.3.cloned.1.call-update) | async-done | bytes 8208 | tf_op jit(solution)/shard_map/reduce_scatter | solution.py:55
  98.7 1.3 multiply_reduce_fusion
  100.0 36.7 %all_gather.6 = f32[8,4096]{1,0:T(8,128)S(1)} all-gather(f32[8,256]{1,0:T(8,128)S(1)} %multiply_subtract_fusion.1), channel_id=1, replica_groups=mesh['section'=2,'dom'=16] {'dom'}, dimensions={1}, use_global_device_ids=true | all-gather | bytes 139264 | tf_op jit(solution)/shard_map/all_gather | solution.py:27
  136.7 1.3 collective-permute-start.1
  138.9 1.4 gather_fusion
  140.3 7.1 %fusion.18 = f32[8,2,1,128,1]{3,2,4,1,0:T(1,128)S(1)} fusion(f32[8,2,6,128,1]{3,4,2,1,0:T(1,128)S(1)} %bitcast.54, f32[8,2,6,128,128]{4,3,2,1,0:T(8,128)} %param.8), kind=kOutput, calls=%fused_computation.40 | convolution fusion | flops 18874368 | bytes 6348800 | tf_op jit(solution)/shard_map/prkij,prkj->pri/dot_general | solution.py:32
  147.4 0.7 multiply_reduce_fusion.1
  148.1 5.1 %fusion.8 = f32[8,2,1,6,128]{4,2,3,1,0:T(1,128)S(1)} fusion(f32[8,2,6,128,128]{4,3,2,1,0:T(8,128)} %param.8, f32[8,2,128,1,1]{2,0,1,3,4:T(8,128)S(1)} %bitcast.57), kind=kOutput, calls=%fused_computation.22 | convolution fusion | flops 18874368 | bytes 6348800 | tf_op jit(solution)/shard_map/prkij,pri->prkj/dot_general | solution.py:42
  153.2 0.9 scatter_custom_fusion.1
  154.1 1.3 collective-permute-start.2
  155.5 1.7 collective-permute-done.2
  157.9 37.2 %all-reduce.2 = (f32[]{:T(128)}, f32[]{:T(128)}) all-reduce(f32[]{:T(128)} %get-tuple-element.8, f32[]{:T(128)} %get-tuple-element.6), channel_id=1, replica_groups=mesh['section'=2,'dom'=16] {'section','dom'}, use_global_device_ids=true, to_apply=%region_3.0 | all-reduce | flops 2 | bytes 16 | tf_op jit(solution)/shard_map/psum | solution.py:76
  196.5 35.8 %reduce-scatter.5.cloned.1.call-done = f32[8,256]{1,0:T(8,128)} async-done(((f32[8,4096]{1,0:T(8,128)}), f32[8,256]{1,0:T(8,128)}) %reduce-scatter.5.cloned.1.call-update) | async-done | bytes 8208 | tf_op jit(solution)/shard_map/reduce_scatter | solution.py:55
  232.3 1.3 multiply_subtract_fusion
  233.6 36.6 %all_gather.7 = f32[8,4096]{1,0:T(8,128)S(1)} all-gather(f32[8,256]{1,0:T(8,128)S(1)} %get-tuple-element.4), channel_id=1, replica_groups=mesh['section'=2,'dom'=16] {'dom'}, dimensions={1}, use_global_device_ids=true | all-gather | bytes 139264 | tf_op jit(solution)/shard_map/all_gather | solution.py:27
  270.3 1.5 collective-permute-start.3
  272.5 1.4 gather_fusion.1
  273.9 7.1 %fusion.19 = f32[8,2,1,128,1]{3,2,4,1,0:T(1,128)S(1)} fusion(f32[8,2,6,128,1]{3,4,2,1,0:T(1,128)S(1)} %bitcast.53, f32[8,2,6,128,128]{4,3,2,1,0:T(8,128)} %param.8), kind=kOutput, calls=%fused_computation.41 | convolution fusion | flops 18874368 | bytes 6348800 | tf_op jit(solution)/shard_map/prkij,prkj->pri/dot_general | solution.py:32
  (40 shorter events, 3.4 us)
Async XLA Ops:
  7.2 91.5 %copy-start.1 = (f32[8,256]{1,0:T(8,128)S(1)}, f32[8,256]{1,0:T(8,128)}, u32[]{:S(2)}) copy-start(f32[8,256]{1,0:T(8,128)} %param.13) | copy-start | bytes 24580
  7.2 91.5 %copy-start.2 = (f32[8,256]{1,0:T(8,128)S(1)}, f32[8,256]{1,0:T(8,128)}, u32[]{:S(2)}) copy-start(f32[8,256]{1,0:T(8,128)} %param.11) | copy-start | bytes 24580
  7.2 91.5 %reduce-scatter.3.cloned.1.call-start = ((), (), s32[]{:S(2)}) async-start(), calls=%async_computation.2 | async-start | bytes 139264 | tf_op jit(solution)/shard_map/reduce_scatter | solution.py:55
  14.3 133.1 %copy-start = (f32[8,256]{1,0:T(8,128)S(1)}, f32[8,256]{1,0:T(8,128)}, u32[]{:S(2)}) copy-start(f32[8,256]{1,0:T(8,128)} %param.14) | copy-start | bytes 24580
  14.3 133.1 %copy-start.3 = (f32[8,256]{1,0:T(8,128)S(1)}, f32[8,256]{1,0:T(8,128)}, u32[]{:S(2)}) copy-start(f32[8,256]{1,0:T(8,128)} %param.12) | copy-start | bytes 24580
  15.2 3.1 %collective-permute-start = (f32[1,4096]{1,0:T(1,128)S(1)}, f32[1,4096]{1,0:T(1,128)S(1)}, u32[]{:S(2)}, u32[]{:S(2)}) collective-permute-start(f32[1,4096]{1,0:T(1,128)S(1)} %bitcast.59), channel_id=1, source_target_pairs={{16,0},{17,1},{18,2},{19,3},{20,4},{21,5},{22,6},{23,7},{24,8},{25... | collective-permute-start | bytes 49160 | tf_op jit(solution)/shard_map/ppermute | solution.py:13
  19.0 213.3 %reduce-scatter.5.cloned.1.call-start = ((), (), s32[]{:S(2)}) async-start(), calls=%async_computation.3 | async-start | bytes 139264 | tf_op jit(solution)/shard_map/reduce_scatter | solution.py:55
  136.7 2.1 collective-permute-start.1
  154.1 3.1 %collective-permute-start.2 = (f32[1,4096]{1,0:T(1,128)S(1)}, f32[1,4096]{1,0:T(1,128)S(1)}, u32[]{:S(2)}, u32[]{:S(2)}) collective-permute-start(f32[1,4096]{1,0:T(1,128)S(1)} %bitcast.60), channel_id=1, source_target_pairs={{16,0},{17,1},{18,2},{19,3},{20,4},{21,5},{22,6},{23,7},{24,8},{25... | collective-permute-start | bytes 49160 | tf_op jit(solution)/shard_map/ppermute | solution.py:13
  270.3 2.1 collective-permute-start.3
Sparse Core Ops, SparseCore 0:
  19.1 79.4 reduce-scatter.2
  158.0 74.2 reduce-scatter.4
where the time goes:
time: 289 us; the launch traced here: 288 us
  waiting for transfers between devices  119 us (41%)
  blocking collectives  110 us (38%)
  matrix products  25.4 us (9%)
  between operations  16.4 us (6%)
  other arithmetic  7.89 us (3%)
  starting transfers between devices  5.42 us (2%)
  local copies, waits for them, and re-layouts  3.43 us (1%)
    reduce_scatter x2, waiting for transfers between devices, adjoint(): result = lax.psum_scatter(merged, 'dom', scatter_dimension=1, tiled=True)  115 us
    all_gather x2, blocking collectives, forward(): gathered = lax.all_gather(field, 'dom', axis=1, tiled=True)  73.3 us
    psum x1, blocking collectives, on_device(): lax.psum((local_primal, local_dual), ('section', 'dom'))  37.2 us
    dot_general x2, matrix products, forward(): jnp.einsum('prkij,prkj->pri', blocks, picked, precision=lax.Precision.HIG...  14.2 us
    dot_general x2, matrix products, adjoint(): jnp.einsum('prkij,pri->prkj', blocks, field_blocks, precision=lax.Precisi...  11.2 us
  transfers between devices with their start and end apart: 6, of which 6 were waited for; matrix products, arithmetic and copies ran while one was open for 0% of the time, Pallas kernels for 0%

commit v1 on v0

--- a/solution.py
+++ b/solution.py
@@ -24,7 +24,15 @@
 def forward(blocks, column_index, slot_index, field):
     periods_here = field.shape[0]
     width_here = blocks.shape[-1]
-    gathered = lax.all_gather(field, "dom", axis=1, tiled=True)
+    ways, here = (lax.axis_size("dom"), lax.axis_index("dom"))
+    grown, reach = (field, 1)
+    while reach < ways:
+        theirs = lax.ppermute(grown, "dom", [(d, d ^ reach) for d in range(ways)])
+        mine_first = jnp.concatenate([grown, theirs], axis=1)
+        theirs_first = jnp.concatenate([theirs, grown], axis=1)
+        grown = jnp.where(here & reach == 0, mine_first, theirs_first)
+        reach = 2 * reach
+    gathered = grown
     carried = passed_along(gathered[-1:], "section", 1)
     stacked = jnp.concatenate([carried, gathered], axis=0)
     block_count = stacked.shape[1] // width_here

time: 289 us -> 248 us (0.86)
  blocking collectives: 110 us -> 37.9 us
  waiting for transfers between devices: 119 us -> 151 us
    all_gather x2 -> x0, blocking collectives: 73.3 us -> none  [forward(): gathered = lax.all_gather(field, 'dom', axis=1, tiled=True)]
    ppermute x0 -> x8, waiting for transfers between devices: none -> 33.2 us  [forward(): theirs = lax.ppermute(grown, 'dom', [(d, d ^ reach) for d in range(ways)])]
  transfers between devices with their start and end apart: 6 -> 14, of which waited for: 6 -> 14; matrix products, arithmetic and copies ran while one was open for 0% -> 0% of each run, Pallas kernels for 0% -> 0%
where the time goes in v1:
time: 248 us
  waiting for transfers between devices  151 us (61%)
  blocking collectives  37.9 us (15%)
  matrix products  25.4 us (10%)
  between operations  16.5 us (7%)
  other arithmetic  7.96 us (3%)
  starting transfers between devices  5.58 us (2%)
  local copies, waits for them, and re-layouts  3.43 us (1%)
    reduce_scatter x2, waiting for transfers between devices, adjoint(): result = lax.psum_scatter(merged, 'dom', scatter_dimension=1, tiled=True)  113 us
    psum x1, blocking collectives, on_device(): lax.psum((local_primal, local_dual), ('section', 'dom'))  37.9 us
    ppermute x8, waiting for transfers between devices, forward(): theirs = lax.ppermute(grown, 'dom', [(d, d ^ reach) for d in range(ways)])  33.2 us
    dot_general x2, matrix products, forward(): jnp.einsum('prkij,prkj->pri', blocks, picked, precision=lax.Precision.HIG...  14.2 us
    dot_general x2, matrix products, adjoint(): jnp.einsum('prkij,pri->prkj', blocks, field_blocks, precision=lax.Precisi...  11.2 us
    ppermute x4, starting transfers between devices, passed_along(): return lax.ppermute(block, axis, route)  5.35 us
  transfers between devices with their start and end apart: 14, of which 14 were waited for; matrix products, arithmetic and copies ran while one was open for 0% of the time, Pallas kernels for 0%

profile of v1, /device:TPU:0, one launch (start us, length us, event | category | flops | bytes accessed | tf_op | source)
XLA Modules:
  0.0 247.8 jit_solution(15452646120881904827)
XLA Ops:
  8.2 6.1 %fusion.10 = f32[8,2,1,6,128]{4,2,3,1,0:T(1,128)S(1)} fusion(f32[8,2,6,128,128]{4,3,2,1,0:T(8,128)} %param.8, f32[8,2,128,1,1]{2,0,1,3,4:T(8,128)} %bitcast.58), kind=kOutput, calls=%fused_computation.32 | convolution fusion | flops 18874368 | bytes 6348800 | tf_op jit(solution)/shard_map/prkij,pri->prkj/dot_general | solution.py:50
  15.3 1.3 collective-permute-start
  16.6 1.7 collective-permute-done
  19.8 78.9 %reduce-scatter.3.cloned.1.call-done = f32[8,256]{1,0:T(8,128)} async-done(((f32[8,4096]{1,0:T(8,128)}), f32[8,256]{1,0:T(8,128)}) %reduce-scatter.3.cloned.1.call-update) | async-done | bytes 8208 | tf_op jit(solution)/shard_map/reduce_scatter | solution.py:63
  98.7 1.3 multiply_reduce_fusion
  100.0 3.6 %collective-permute-done.1 = f32[8,256]{1,0:T(8,128)S(1)} collective-permute-done((f32[8,256]{1,0:T(8,128)S(1)}, f32[8,256]{1,0:T(8,128)S(1)}, u32[]{:S(2)}, u32[]{:S(2)}) %collective-permute-start.1) | collective-permute-done | bytes 8224 | tf_op jit(solution)/shard_map/ppermute | solution.py:30
  103.7 3.7 %collective-permute-done.2 = f32[8,512]{1,0:T(8,128)S(1)} collective-permute-done((f32[8,512]{1,0:T(8,128)S(1)}, f32[8,512]{1,0:T(8,128)S(1)}, u32[]{:S(2)}, u32[]{:S(2)}) %collective-permute-start.2) | collective-permute-done | bytes 16416 | tf_op jit(solution)/shard_map/ppermute | solution.py:30
  107.4 3.9 %collective-permute-done.3 = f32[8,1024]{1,0:T(8,128)S(1)} collective-permute-done((f32[8,1024]{1,0:T(8,128)S(1)}, f32[8,1024]{1,0:T(8,128)S(1)}, u32[]{:S(2)}, u32[]{:S(2)}) %collective-permute-start.3) | collective-permute-done | bytes 32800 | tf_op jit(solution)/shard_map/ppermute | solution.py:30
  111.4 5.3 %collective-permute-done.4 = f32[8,2048]{1,0:T(8,128)S(1)} collective-permute-done((f32[8,2048]{1,0:T(8,128)S(1)}, f32[8,2048]{1,0:T(8,128)S(1)}, u32[]{:S(2)}, u32[]{:S(2)}) %collective-permute-start.4) | collective-permute-done | bytes 65568 | tf_op jit(solution)/shard_map/ppermute | solution.py:30
  119.0 1.4 gather_fusion
  120.4 7.1 %fusion.18 = f32[8,2,1,128,1]{3,2,4,1,0:T(1,128)S(1)} fusion(f32[8,2,6,128,1]{3,4,2,1,0:T(1,128)S(1)} %bitcast.54, f32[8,2,6,128,128]{4,3,2,1,0:T(8,128)} %param.8), kind=kOutput, calls=%fused_computation.48 | convolution fusion | flops 18874368 | bytes 6348800 | tf_op jit(solution)/shard_map/prkij,prkj->pri/dot_general | solution.py:40
  128.1 5.1 %fusion.8 = f32[8,2,1,6,128]{4,2,3,1,0:T(1,128)S(1)} fusion(f32[8,2,6,128,128]{4,3,2,1,0:T(8,128)} %param.8, f32[8,2,128,1,1]{2,0,1,3,4:T(8,128)S(1)} %bitcast.57), kind=kOutput, calls=%fused_computation.30 | convolution fusion | flops 18874368 | bytes 6348800 | tf_op jit(solution)/shard_map/prkij,pri->prkj/dot_general | solution.py:50
  134.2 1.3 collective-permute-start.6
  135.5 1.7 collective-permute-done.6
  138.0 37.9 %all-reduce.2 = (f32[]{:T(128)}, f32[]{:T(128)}) all-reduce(f32[]{:T(128)} %get-tuple-element.8, f32[]{:T(128)} %get-tuple-element.6), channel_id=1, replica_groups=mesh['section'=2,'dom'=16] {'section','dom'}, use_global_device_ids=true, to_apply=%region_3.4 | all-reduce | flops 2 | bytes 16 | tf_op jit(solution)/shard_map/psum | solution.py:84
  177.3 34.3 %reduce-scatter.5.cloned.1.call-done = f32[8,256]{1,0:T(8,128)} async-done(((f32[8,4096]{1,0:T(8,128)}), f32[8,256]{1,0:T(8,128)}) %reduce-scatter.5.cloned.1.call-update) | async-done | bytes 8208 | tf_op jit(solution)/shard_map/reduce_scatter | solution.py:63
  211.6 1.3 multiply_subtract_fusion
  212.9 3.6 %collective-permute-done.7 = f32[8,256]{1,0:T(8,128)S(1)} collective-permute-done((f32[8,256]{1,0:T(8,128)S(1)}, f32[8,256]{1,0:T(8,128)S(1)}, u32[]{:S(2)}, u32[]{:S(2)}) %collective-permute-start.7) | collective-permute-done | bytes 8224 | tf_op jit(solution)/shard_map/ppermute | solution.py:30
  216.6 3.7 %collective-permute-done.8 = f32[8,512]{1,0:T(8,128)S(1)} collective-permute-done((f32[8,512]{1,0:T(8,128)S(1)}, f32[8,512]{1,0:T(8,128)S(1)}, u32[]{:S(2)}, u32[]{:S(2)}) %collective-permute-start.8) | collective-permute-done | bytes 16416 | tf_op jit(solution)/shard_map/ppermute | solution.py:30
  220.3 3.9 %collective-permute-done.9 = f32[8,1024]{1,0:T(8,128)S(1)} collective-permute-done((f32[8,1024]{1,0:T(8,128)S(1)}, f32[8,1024]{1,0:T(8,128)S(1)}, u32[]{:S(2)}, u32[]{:S(2)}) %collective-permute-start.9) | collective-permute-done | bytes 32800 | tf_op jit(solution)/shard_map/ppermute | solution.py:30
  224.3 5.3 %collective-permute-done.10 = f32[8,2048]{1,0:T(8,128)S(1)} collective-permute-done((f32[8,2048]{1,0:T(8,128)S(1)}, f32[8,2048]{1,0:T(8,128)S(1)}, u32[]{:S(2)}, u32[]{:S(2)}) %collective-permute-start.10) | collective-permute-done | bytes 65568 | tf_op jit(solution)/shard_map/ppermute | solution.py:30
  229.6 1.5 collective-permute-start.11
  231.9 1.4 gather_fusion.1
  233.3 7.1 %fusion.19 = f32[8,2,1,128,1]{3,2,4,1,0:T(1,128)S(1)} fusion(f32[8,2,6,128,1]{3,4,2,1,0:T(1,128)S(1)} %bitcast.53, f32[8,2,6,128,128]{4,3,2,1,0:T(8,128)} %param.8), kind=kOutput, calls=%fused_computation.49 | convolution fusion | flops 18874368 | bytes 6348800 | tf_op jit(solution)/shard_map/prkij,prkj->pri/dot_general | solution.py:40
  (62 shorter events, 8.8 us)
Async XLA Ops:
  7.2 91.5 %copy-start.1 = (f32[8,256]{1,0:T(8,128)S(1)}, f32[8,256]{1,0:T(8,128)}, u32[]{:S(2)}) copy-start(f32[8,256]{1,0:T(8,128)} %param.13) | copy-start | bytes 24580
  7.2 91.5 %copy-start.2 = (f32[8,256]{1,0:T(8,128)S(1)}, f32[8,256]{1,0:T(8,128)}, u32[]{:S(2)}) copy-start(f32[8,256]{1,0:T(8,128)} %param.11) | copy-start | bytes 24580
  7.2 91.5 %reduce-scatter.3.cloned.1.call-start = ((), (), s32[]{:S(2)}) async-start(), calls=%async_computation.2 | async-start | bytes 139264 | tf_op jit(solution)/shard_map/reduce_scatter | solution.py:63
  14.3 113.2 %copy-start = (f32[8,256]{1,0:T(8,128)S(1)}, f32[8,256]{1,0:T(8,128)}, u32[]{:S(2)}) copy-start(f32[8,256]{1,0:T(8,128)} %param.14) | copy-start | bytes 24580
  14.3 113.2 %copy-start.3 = (f32[8,256]{1,0:T(8,128)S(1)}, f32[8,256]{1,0:T(8,128)}, u32[]{:S(2)}) copy-start(f32[8,256]{1,0:T(8,128)} %param.12) | copy-start | bytes 24580
  15.3 3.1 %collective-permute-start = (f32[1,4096]{1,0:T(1,128)S(1)}, f32[1,4096]{1,0:T(1,128)S(1)}, u32[]{:S(2)}, u32[]{:S(2)}) collective-permute-start(f32[1,4096]{1,0:T(1,128)S(1)} %bitcast.59), channel_id=1, source_target_pairs={{16,0},{17,1},{18,2},{19,3},{20,4},{21,5},{22,6},{23,7},{24,8},{25... | collective-permute-start | bytes 49160 | tf_op jit(solution)/shard_map/ppermute | solution.py:13
  19.0 192.6 %reduce-scatter.5.cloned.1.call-start = ((), (), s32[]{:S(2)}) async-start(), calls=%async_computation.3 | async-start | bytes 139264 | tf_op jit(solution)/shard_map/reduce_scatter | solution.py:63
  100.0 3.7 %collective-permute-start.1 = (f32[8,256]{1,0:T(8,128)S(1)}, f32[8,256]{1,0:T(8,128)S(1)}, u32[]{:S(2)}, u32[]{:S(2)}) collective-permute-start(f32[8,256]{1,0:T(8,128)S(1)} %multiply_subtract_fusion.1), channel_id=1, source_target_pairs={{0,1},{1,0},{2,3},{3,2},{4,5},{5,4},{6,7},{7,6},{8,9},{9,8},{10,11... | collective-permute-start | bytes 24584 | tf_op jit(solution)/shard_map/ppermute | solution.py:30
  103.7 3.7 %collective-permute-start.2 = (f32[8,512]{1,0:T(8,128)S(1)}, f32[8,512]{1,0:T(8,128)S(1)}, u32[]{:S(2)}, u32[]{:S(2)}) collective-permute-start(f32[8,512]{1,0:T(8,128)S(1)} %maximum_select_fusion.6), channel_id=1, source_target_pairs={{0,2},{1,3},{2,0},{3,1},{4,6},{5,7},{6,4},{7,5},{8,10},{9,11},{10,... | collective-permute-start | bytes 49160 | tf_op jit(solution)/shard_map/ppermute | solution.py:30
  107.4 3.9 %collective-permute-start.3 = (f32[8,1024]{1,0:T(8,128)S(1)}, f32[8,1024]{1,0:T(8,128)S(1)}, u32[]{:S(2)}, u32[]{:S(2)}) collective-permute-start(f32[8,1024]{1,0:T(8,128)S(1)} %maximum_select_fusion.4), channel_id=1, source_target_pairs={{0,4},{1,5},{2,6},{3,7},{4,0},{5,1},{6,2},{7,3},{8,12},{9,13},{10,... | collective-permute-start | bytes 98312 | tf_op jit(solution)/shard_map/ppermute | solution.py:30
  111.3 5.4 %collective-permute-start.4 = (f32[8,2048]{1,0:T(8,128)S(1)}, f32[8,2048]{1,0:T(8,128)S(1)}, u32[]{:S(2)}, u32[]{:S(2)}) collective-permute-start(f32[8,2048]{1,0:T(8,128)S(1)} %maximum_select_fusion.2), channel_id=1, source_target_pairs={{0,8},{1,9},{2,10},{3,11},{4,12},{5,13},{6,14},{7,15},{8,0},{9,1},... | collective-permute-start | bytes 196616 | tf_op jit(solution)/shard_map/ppermute | solution.py:30
  116.7 2.1 collective-permute-start.5
  134.2 3.1 %collective-permute-start.6 = (f32[1,4096]{1,0:T(1,128)S(1)}, f32[1,4096]{1,0:T(1,128)S(1)}, u32[]{:S(2)}, u32[]{:S(2)}) collective-permute-start(f32[1,4096]{1,0:T(1,128)S(1)} %bitcast.60), channel_id=1, source_target_pairs={{16,0},{17,1},{18,2},{19,3},{20,4},{21,5},{22,6},{23,7},{24,8},{25... | collective-permute-start | bytes 49160 | tf_op jit(solution)/shard_map/ppermute | solution.py:13
  212.9 3.7 %collective-permute-start.7 = (f32[8,256]{1,0:T(8,128)S(1)}, f32[8,256]{1,0:T(8,128)S(1)}, u32[]{:S(2)}, u32[]{:S(2)}) collective-permute-start(f32[8,256]{1,0:T(8,128)S(1)} %get-tuple-element.4), channel_id=1, source_target_pairs={{0,1},{1,0},{2,3},{3,2},{4,5},{5,4},{6,7},{7,6},{8,9},{9,8},{10,11... | collective-permute-start | bytes 24584 | tf_op jit(solution)/shard_map/ppermute | solution.py:30
  216.6 3.7 %collective-permute-start.8 = (f32[8,512]{1,0:T(8,128)S(1)}, f32[8,512]{1,0:T(8,128)S(1)}, u32[]{:S(2)}, u32[]{:S(2)}) collective-permute-start(f32[8,512]{1,0:T(8,128)S(1)} %maximum_select_fusion.7), channel_id=1, source_target_pairs={{0,2},{1,3},{2,0},{3,1},{4,6},{5,7},{6,4},{7,5},{8,10},{9,11},{10,... | collective-permute-start | bytes 49160 | tf_op jit(solution)/shard_map/ppermute | solution.py:30
  220.3 3.9 %collective-permute-start.9 = (f32[8,1024]{1,0:T(8,128)S(1)}, f32[8,1024]{1,0:T(8,128)S(1)}, u32[]{:S(2)}, u32[]{:S(2)}) collective-permute-start(f32[8,1024]{1,0:T(8,128)S(1)} %maximum_select_fusion.5), channel_id=1, source_target_pairs={{0,4},{1,5},{2,6},{3,7},{4,0},{5,1},{6,2},{7,3},{8,12},{9,13},{10,... | collective-permute-start | bytes 98312 | tf_op jit(solution)/shard_map/ppermute | solution.py:30
  224.2 5.4 %collective-permute-start.10 = (f32[8,2048]{1,0:T(8,128)S(1)}, f32[8,2048]{1,0:T(8,128)S(1)}, u32[]{:S(2)}, u32[]{:S(2)}) collective-permute-start(f32[8,2048]{1,0:T(8,128)S(1)} %maximum_select_fusion.3), channel_id=1, source_target_pairs={{0,8},{1,9},{2,10},{3,11},{4,12},{5,13},{6,14},{7,15},{8,0},{9,1},... | collective-permute-start | bytes 196616 | tf_op jit(solution)/shard_map/ppermute | solution.py:30
  229.6 2.1 collective-permute-start.11
Sparse Core Ops, SparseCore 0:
  19.1 79.4 reduce-scatter.2
  138.1 73.4 reduce-scatter.4
